TPU v7x, 256 devices: a whole 4x4x8 slice. The times are simulated.
256 devices in a mesh: grp: 16 (over z, core), pts: 16 (over y, x).
Axes of the slice: x: 4, y: 4, z: 8, core: 2. Of those that a mesh axis runs over, the one named last changes fastest.
Arguments:
- patches: bfloat16 [16, 16, 16384, 128], P('grp', 'pts'), may hold values from -6 to 6
- counts: int32 [16, 16], replicated, may hold values from 1 to 16384, as said below
- pick_slot: int32 [3, 128], replicated, may hold values from 0 to 16383, as said below
- block_owner: int32 [3], replicated, may hold values from 0 to 255, as said below
Outputs:
- factor_rows: bfloat16 [16, 16, 8192, 384], P('grp', 'pts')
- residual_gain: float32 [16, 16, 8192], P('grp', 'pts')
Inputs may be any that keep to these rules, and one draw needn't show every extreme that they name: `counts`: each row sums to 131072, and in every row one device holds exactly 16384; in the last row it is the last column. `pick_slot`: the 128 slots of round r are distinct and below the count of block_owner[r]; the round owned by the last device includes slot 16383. `block_owner`: the owners of the rounds are distinct devices, and one of them is the last device.
All inputs are finite; a program needn't handle non-finite values.
Results may differ from a plain program's by a relative error of at most 0.0075.
Values may be sent and summed in bfloat16 or wider, within the bound.
A program may use at most 192 MiB of HBM per device.

v0:
```python
import jax
import jax.numpy as jnp
from jax import lax
from jax.sharding import PartitionSpec as P

PTS_DEV = 8192
JITTER = 0.1
HIGHEST = lax.Precision.HIGHEST


def from_root(block, axis, holder):
    block = jnp.where(lax.axis_index(axis) == holder, block, jnp.zeros_like(block))
    return lax.psum(block, axis)


def squares(matrix):
    return jnp.sum(jnp.square(matrix.astype(jnp.float32)), axis=1)


def affinity(row_data, rows_sq, row_ids, block_rows, block_sq, block_ids):
    cross_dot = lax.dot_general(
        row_data, block_rows, (((1,), (1,)), ((), ())), preferred_element_type=jnp.float32
    )
    inverse_scale = 1.0 / row_data.shape[1]
    distance = rows_sq[:, None] + block_sq[None, :] - 2.0 * cross_dot
    same_point = (row_ids[:, None] == block_ids[None, :]).astype(jnp.float32)
    return jnp.exp(-inverse_scale * distance) + JITTER * same_point


def extend(factors, kernel_part, cross_rows, inverse):
    if factors.shape[1] > 0:
        kernel_part = kernel_part - lax.dot_general(
            factors,
            cross_rows,
            (((1,), (1,)), ((), ())),
            precision=HIGHEST,
            preferred_element_type=jnp.float32,
        )
    fresh_rows = lax.dot_general(
        kernel_part,
        inverse,
        (((1,), (1,)), ((), ())),
        precision=HIGHEST,
        preferred_element_type=jnp.float32,
    )
    return jnp.concatenate([factors, fresh_rows], axis=1)


def prepare(blocks, block_ids):
    round_count, block_size = block_ids.shape
    stacked = blocks.reshape(round_count * block_size, blocks.shape[2])
    stacked_ids = block_ids.reshape(-1)
    stacked_sq = squares(stacked)
    factors = jnp.zeros((round_count * block_size, 0), jnp.float32)
    identity = jnp.eye(block_size, dtype=jnp.float32)
    inverses = []
    crosses = []
    for step_index in range(round_count):
        lower_edge = step_index * block_size
        cross_rows = factors[lower_edge : lower_edge + block_size]
        block_sq = stacked_sq[lower_edge : lower_edge + block_size]
        schur_block = affinity(
            blocks[step_index],
            block_sq,
            block_ids[step_index],
            blocks[step_index],
            block_sq,
            block_ids[step_index],
        )
        if step_index > 0:
            schur_block = schur_block - lax.dot_general(
                cross_rows,
                cross_rows,
                (((1,), (1,)), ((), ())),
                precision=HIGHEST,
                preferred_element_type=jnp.float32,
            )
        factor_low = jnp.linalg.cholesky(schur_block)
        inverse = lax.linalg.triangular_solve(factor_low, identity, left_side=True, lower=True)
        kernel_part = affinity(
            stacked, stacked_sq, stacked_ids, blocks[step_index], block_sq, block_ids[step_index]
        )
        factors = extend(factors, kernel_part, cross_rows, inverse)
        inverses.append(inverse)
        crosses.append(cross_rows)
    return (inverses, crosses)


def factorize(row_data, row_ids, blocks, block_ids, inverses, crosses):
    rows_sq = squares(row_data)
    blocks_sq = squares(blocks.reshape(-1, blocks.shape[2])).reshape(block_ids.shape)
    factors = jnp.zeros((row_data.shape[0], 0), jnp.float32)
    for step_index in range(len(inverses)):
        kernel_part = affinity(
            row_data,
            rows_sq,
            row_ids,
            blocks[step_index],
            blocks_sq[step_index],
            block_ids[step_index],
        )
        factors = extend(factors, kernel_part, crosses[step_index], inverses[step_index])
    point_gains = 1.0 + JITTER - jnp.sum(factors * factors, axis=1)
    return (factors, point_gains)


def per_device(patches, counts, pick_slot, block_owner):
    groups = lax.axis_size("grp")
    columns = lax.axis_size("pts")
    my_group = lax.axis_index("grp")
    my_column = lax.axis_index("pts")
    local_rows = patches[0, 0]
    slot_count = local_rows.shape[0]
    embed_width = local_rows.shape[1]
    per_peer = slot_count // groups
    round_count, block_size = pick_slot.shape
    ends_table = jnp.cumsum(counts, axis=1)
    starts_table = ends_table - counts
    col_ends = lax.dynamic_index_in_dim(ends_table, my_column, 0, keepdims=False)
    col_starts = lax.dynamic_index_in_dim(starts_table, my_column, 0, keepdims=False)
    my_start = lax.dynamic_index_in_dim(col_starts, my_group, 0, keepdims=False)
    my_count = lax.dynamic_index_in_dim(col_ends, my_group, 0, keepdims=False) - my_start
    target = jnp.arange(groups, dtype=jnp.int32)[:, None]
    offsets = (target - my_start) % groups + jnp.arange(per_peer, dtype=jnp.int32)[None, :] * groups
    in_range = offsets < my_count
    take_rows = jnp.minimum(offsets, slot_count - 1).reshape(-1)
    slot_rank = jnp.arange(PTS_DEV, dtype=jnp.int32) * groups + my_group
    sources = jnp.sum((col_ends[None, :] <= slot_rank[:, None]).astype(jnp.int32), axis=1)
    begin_slot = (col_starts + (my_group - col_starts) % groups) // groups
    source_hit = jnp.arange(groups, dtype=jnp.int32)[None, :] == sources[:, None]
    source_begin = jnp.sum(jnp.where(source_hit, begin_slot[None, :], 0), axis=1)
    take_index = sources * per_peer + jnp.arange(PTS_DEV, dtype=jnp.int32) - source_begin
    owner_group = block_owner // columns
    owner_column = block_owner % columns
    pick_rank = starts_table[owner_column, owner_group][:, None] + pick_slot
    block_ids = (
        pick_rank % groups * columns + owner_column[:, None]
    ) * PTS_DEV + pick_rank // groups
    chosen = jnp.take(local_rows, pick_slot.reshape(-1), axis=0).reshape(
        round_count, block_size, embed_width
    )
    fetched = []
    for step_index in range(round_count):
        fetched.append(from_root(chosen[step_index], ("grp", "pts"), block_owner[step_index]))
    blocks = jnp.stack(fetched)
    inverses, crosses = prepare(blocks, block_ids)
    shaped = jnp.take(local_rows, take_rows, axis=0).reshape(
        (groups, per_peer) + local_rows.shape[1:]
    )
    keep_mask = in_range.reshape((groups, per_peer) + (1,) * (local_rows.ndim - 1))
    received = lax.all_to_all(
        jnp.where(keep_mask, shaped, jnp.zeros((), local_rows.dtype)),
        "grp",
        split_axis=0,
        concat_axis=0,
        tiled=True,
    )
    flat_rows = received.reshape((groups * per_peer,) + received.shape[2:])
    points = jnp.take(flat_rows, take_index, axis=0)
    point_ids = (my_group * columns + my_column) * PTS_DEV + jnp.arange(PTS_DEV, dtype=jnp.int32)
    factors, point_gains = factorize(points, point_ids, blocks, block_ids, inverses, crosses)
    factor_rows = factors.astype(jnp.bfloat16)
    return (factor_rows[None, None], point_gains[None, None])


def solution(mesh):
    in_specs = (P("grp", "pts", None, None), P(), P(), P())
    out_specs = (P("grp", "pts", None, None), P("grp", "pts", None))
    return jax.shard_map(
        per_device, mesh=mesh, in_specs=in_specs, out_specs=out_specs, check_vma=False
    )
```

profile of v0, /device:TPU:1, one launch (start us, length us, event | category | flops | bytes accessed | tf_op | source)
XLA Modules:
  0.0 556.6 jit_solution(17895677158123767266)
XLA Ops:
  7.2 0.9 reduce_window_sum.11
  8.0 0.7 sub.107
  8.7 0.6 dynamic_slice.17
  9.3 0.6 dynamic_slice.16
  9.9 0.7 and_select_fusion.2
  12.2 58.2 %gather_fusion = bf16[16384,128]{1,0:T(8,128)(2,1)} fusion(bf16[16384,128]{1,0:T(8,128)(2,1)} %bitcast.108, s32[16384]{0:T(1024)S(1)} %broadcast_clamp_fusion), kind=kCustom, calls=%fused_computation | custom fusion | bytes 8454144 | tf_op jit(solution)/shard_map/jit(_take)/gather | solution.py:147
  70.4 7.6 %select_select_fusion = bf16[16,1024,128]{2,1,0:T(8,128)(2,1)} fusion(bf16[16,1024,128]{2,1,0:T(8,128)(2,1)} %bitcast.110, pred[16,1024]{1,0:T(8,128)(4,1)S(1)} %get-tuple-element.21, pred[16,1024]{1,0:T(8,128)(4,1)S(1)} %get-tuple-element.20), kind=kLoop, calls=%fused_computation.28 | loop fusion | flops 4194304 | bytes 8421376 | tf_op jit(solution)/shard_map/jit(_where)/select_n | solution.py:152
  78.0 10.1 %all-to-all-start = ((bf16[16,1024,128]{2,1,0:T(8,128)(2,1)}), bf16[16,1024,128]{2,1,0:T(8,128)(2,1)}, u32[]{:S(2)}, u32[]{:S(2)}) async-start(bf16[16,1024,128]{2,1,0:T(8,128)(2,1)} %select_select_fusion), calls=%async_computation | async-start | bytes 8388608 | tf_op jit(solution)/shard_map/all_to_all | solution.py:151
  88.2 0.6 fusion.77
  90.8 4.2 gather_fusion.2
  95.1 0.6 slice_select_fusion.2
  95.8 0.6 gather_fusion.3
  97.1 284.2 %all-reduce.3.cloned.1.call-done = (bf16[128,128]{1,0:T(8,128)(2,1)}, bf16[128,128]{1,0:T(8,128)(2,1)}, bf16[128,128]{1,0:T(8,128)(2,1)}) async-done(((bf16[128,128]{1,0:T(8,128)(2,1)}, bf16[128,128]{1,0:T(8,128)(2,1)}, bf16[128,128]{1,0:T(8,128)(2,1)}), (bf16[128,128]{1,0:T(8,128)(2,1)}, bf16[128,128]{1,0:T(8,128)(2,1)}, bf16[128,128]{1,0:T(8,128)(2,1)})) %all-reduce.3.cloned.1.call-update) | async-done | bytes 98320 | tf_op jit(solution)/shard_map/psum | solution.py:13
  381.4 0.9 multiply_reduce_fusion.1
  382.3 1.0 fusion.36
  383.5 11.7 %cholesky.59 = f32[128,128]{1,0:T(8,128)S(1)} custom-call(f32[128,128]{1,0:T(8,128)S(1)} %fusion.54), custom_call_target="Cholesky" | custom-call | tf_op jit(solution)/shard_map/jit(cholesky)/cholesky | solution.py:78
  395.2 0.6 compare_reduce_fusion.2
  395.9 0.7 fusion.46
  396.5 9.8 %custom-call.9 = f32[1,128,128]{1,2,0:T(8,128)S(1)} custom-call(f32[1,128,128]{2,1,0:T(8,128)S(1)} %fusion.46), custom_call_target="InvertDiagBlocksLowerTriangular" | custom-call | tf_op jit(solution)/shard_map/triangular_solve/custom-call.0 | solution.py:79
  406.6 1.0 fusion.32
  407.6 1.0 fusion.19
  408.6 0.4 fusion.79
  409.4 11.7 %cholesky.70 = f32[128,128]{1,0:T(8,128)S(1)} custom-call(f32[128,128]{1,0:T(8,128)S(1)} %fusion.52), custom_call_target="Cholesky" | custom-call | tf_op jit(solution)/shard_map/jit(cholesky)/cholesky | solution.py:78
  421.2 0.6 compare_reduce_fusion.1
  421.8 0.7 fusion.47
  422.5 10.3 %custom-call.10 = f32[1,128,128]{1,2,0:T(8,128)S(1)} custom-call(f32[1,128,128]{2,1,0:T(8,128)S(1)} %fusion.47), custom_call_target="InvertDiagBlocksLowerTriangular" | custom-call | tf_op jit(solution)/shard_map/triangular_solve/custom-call.0 | solution.py:79
  433.1 1.0 fusion.28
  434.1 0.5 fusion.56
  434.6 1.0 fusion.24
  435.6 0.4 fusion.81
  436.5 11.7 %cholesky.81 = f32[128,128]{1,0:T(8,128)S(1)} custom-call(f32[128,128]{1,0:T(8,128)S(1)} %fusion.50), custom_call_target="Cholesky" | custom-call | tf_op jit(solution)/shard_map/jit(cholesky)/cholesky | solution.py:78
  448.2 0.6 compare_reduce_fusion
  448.9 0.7 fusion.48
  449.5 9.8 %custom-call.11 = f32[1,128,128]{1,2,0:T(8,128)S(1)} custom-call(f32[1,128,128]{2,1,0:T(8,128)S(1)} %fusion.48), custom_call_target="InvertDiagBlocksLowerTriangular" | custom-call | tf_op jit(solution)/shard_map/triangular_solve/custom-call.0 | solution.py:79
  459.7 24.6 %gather_fusion.1 = bf16[8192,128]{1,0:T(8,128)(2,1)S(1)} fusion(bf16[16384,128]{1,0:T(8,128)(2,1)} %bitcast.7, s32[8192]{0:T(1024)S(1)} %broadcast_clamp_fusion.1), kind=kCustom, calls=%fused_computation.1 | custom fusion | bytes 4227072 | tf_op jit(solution)/shard_map/jit(_take)/gather | solution.py:159
  484.3 2.7 multiply_reduce_fusion
  487.0 3.3 fusion.6
  490.4 3.3 fusion.9
  493.7 3.3 fusion.12
  497.1 4.4 fusion.78
  501.5 6.7 %convolution_subtract_fusion.1 = f32[8192,128]{1,0:T(8,128)S(1)} fusion(f32[8192,128]{1,0:T(8,128)S(1)} %fusion.9, f32[8192,128]{0,1:T(8,128)S(1)} %fusion.78, f32[384,128]{0,1:T(8,128)S(1)} %fusion.79), kind=kOutput, calls=%fused_computation.9 | convolution fusion | flops 1611661312 | bytes 12648448 | tf_op jit(solution)/shard_map/dot_general | solution.py:32
  508.2 4.6 fusion.80
  512.8 14.2 %convolution_subtract_fusion = f32[8192,128]{1,0:T(8,128)S(1)} fusion(f32[8192,128]{1,0:T(8,128)S(1)} %fusion.12, f32[8192,128]{0,1:T(8,128)S(1)} %fusion.80, f32[8192,128]{0,1:T(8,128)S(1)} %fusion.78, f32[384,128]{0,1:T(8,128)S(1)} %fusion.81, f32[384,128]{0,1:T(8,128)S(1)} %fusion.79), kind=kOutput, calls=%fused_computation.6 | convolution fusion | flops 3224403968 | bytes 17170432 | tf_op jit(solution)/shard_map/dot_general | solution.py:32
  527.1 4.1 fusion.82
  531.2 1.4 fusion
  533.4 0.6 broadcast_subtract_fusion
  534.0 7.0 %pad_maximum_fusion = bf16[1,1,8192,384]{2,3,1,0:T(8,128)(2,1)} fusion(bf16[1,1,8192,128]{2,3,1,0:T(8,128)(2,1)S(1)} %convert_bitcast_fusion, bf16[1,1,8192,128]{2,3,1,0:T(8,128)(2,1)S(1)} %convert_bitcast_fusion.1, bf16[1,1,8192,128]{2,3,1,0:T(8,128)(2,1)S(1)} %convert_bitcast_fusion.2), kind=kLoop, calls=%fused_computation.26 | loop fusion | flops 18874368 | bytes 12582912 | tf_op jit(solution)/shard_map/concatenate | solution.py:46
  540.9 8.6 %copy.32 = bf16[1,1,8192,384]{3,2,1,0:T(8,128)(2,1)} copy(bf16[1,1,8192,384]{2,3,1,0:T(8,128)(2,1)} %pad_maximum_fusion) | data formatting | bytes 12582912
  (54 shorter events, 3.9 us)
Async XLA Ops:
  78.0 10.2 %copy-start.4 = (s32[3]{0:T(128)S(1)}, s32[3]{0:T(128)}, u32[]{:S(2)}) copy-start(s32[3]{0:T(128)} %param.10) | copy-start | bytes 40
  78.0 12.7 %copy-start.3 = (s32[3,128]{1,0:T(4,128)S(1)}, s32[3,128]{1,0:T(4,128)}, u32[]{:S(2)}) copy-start(s32[3,128]{1,0:T(4,128)} %param.9) | copy-start | bytes 4612
  78.0 381.6 %all-to-all-start = ((bf16[16,1024,128]{2,1,0:T(8,128)(2,1)}), bf16[16,1024,128]{2,1,0:T(8,128)(2,1)}, u32[]{:S(2)}, u32[]{:S(2)}) async-start(bf16[16,1024,128]{2,1,0:T(8,128)(2,1)} %select_select_fusion), calls=%async_computation | async-start | bytes 8388608 | tf_op jit(solution)/shard_map/all_to_all | solution.py:151
  88.2 293.2 %all-reduce.3.cloned.1.call-start = ((), (), s32[]{:S(2)}) async-start(), calls=%async_computation.1 | async-start | bytes 196608 | tf_op jit(solution)/shard_map/psum | solution.py:13
  459.6 27.4 %copy-start.2 = (bf16[128,128]{1,0:T(8,128)(2,1)S(1)}, bf16[128,128]{1,0:T(8,128)(2,1)}, u32[]{:S(2)}) copy-start(bf16[128,128]{1,0:T(8,128)(2,1)} %get-tuple-element.12) | copy-start | bytes 98308
  487.0 3.3 copy-start.1
  490.4 3.3 copy-start
Sparse Core Ops, SparseCore 0:
  95.9 285.4 all-reduce.2
where the time goes:
time: 560 us; the launch traced here: 557 us
  waiting for transfers between devices  284 us (51%)
  local copies, waits for them, and re-layouts  98.4 us (18%)
  other arithmetic  94 us (17%)
  matrix products  51.8 us (9%)
  between operations  17.9 us (3%)
  starting transfers between devices  10.2 us (2%)
    psum x1, waiting for transfers between devices, from_root(): return lax.psum(block, axis)  284 us
    gather x1, local copies, waits for them, and re-layouts, per_device(): jnp.take(local_rows, take_rows, axis=0)  58.2 us
    another operation x9, other arithmetic, prepare(): factor_low = jnp.linalg.cholesky(schur_block)  37.2 us
    another operation x6, other arithmetic, prepare(): lax.linalg.triangular_solve(factor_low, identity, left_side=True, lower=T...  31.9 us
    gather x1, local copies, waits for them, and re-layouts, per_device(): points = jnp.take(flat_rows, take_index, axis=0)  24.6 us
    dot_general x3, matrix products, extend(): lax.dot_general(factors, cross_rows, (((1,), (1,)), ((), ())), precision=...  21.4 us
    dot_general x8, matrix products, affinity(): lax.dot_general(row_data, block_rows, (((1,), (1,)), ((), ())), preferred...  14.9 us
    dot_general x5, matrix products, extend(): lax.dot_general(kernel_part, inverse, (((1,), (1,)), ((), ())), precision...  14 us
  transfers between devices with their start and end apart: 2, of which 1 were waited for; matrix products, arithmetic and copies ran while one was open for 15% of the time, Pallas kernels for 0%

commit v1 on v0

--- a/solution.py
+++ b/solution.py
@@ -10,7 +10,7 @@
 
 def from_root(block, axis, holder):
     block = jnp.where(lax.axis_index(axis) == holder, block, jnp.zeros_like(block))
-    return lax.psum(block, axis)
+    return jnp.sum(lax.all_gather(block, axis), axis=0)
 
 
 def squares(matrix):

time: 560 us -> 597 us (1.066)
  matrix products: 51.8 us -> 68.1 us
  other arithmetic: 94 us -> 108 us
    psum x1 -> x0, waiting for transfers between devices: 284 us -> none  [from_root(): return lax.psum(block, axis)]
    all_gather x0 -> x3, waiting for transfers between devices: none -> 177 us  [from_root(): return jnp.sum(lax.all_gather(block, axis), axis=0)]
    all_to_all x1, waiting for transfers between devices: 0.01 us -> 106 us  [per_device(): lax.all_to_all(jnp.where(keep_mask, shaped, jnp.zeros((), local_rows.dtyp...]
    dot_general x8, matrix products: 14.9 us -> 29.9 us  [affinity(): lax.dot_general(row_data, block_rows, (((1,), (1,)), ((), ())), preferred...]
    reduce_sum x0 -> x3, other arithmetic: none -> 14.2 us  [from_root(): return jnp.sum(lax.all_gather(block, axis), axis=0)]
  transfers between devices with their start and end apart: 2 -> 4, of which waited for: 1 -> 3; matrix products, arithmetic and copies ran while one was open for 15% -> 18% of each run, Pallas kernels for 0% -> 0%
where the time goes in v1:
time: 597 us; the launch traced here: 588 us
  waiting for transfers between devices  285 us (48%)
  other arithmetic  108 us (18%)
  local copies, waits for them, and re-layouts  98.9 us (17%)
  matrix products  68.1 us (11%)
  between operations  17.9 us (3%)
  starting transfers between devices  10.2 us (2%)
    all_gather x3, waiting for transfers between devices, from_root(): return jnp.sum(lax.all_gather(block, axis), axis=0)  177 us
    all_to_all x1, waiting for transfers between devices, per_device(): lax.all_to_all(jnp.where(keep_mask, shaped, jnp.zeros((), local_rows.dtyp...  106 us
    gather x1, local copies, waits for them, and re-layouts, per_device(): jnp.take(local_rows, take_rows, axis=0)  58.2 us
    another operation x9, other arithmetic, prepare(): factor_low = jnp.linalg.cholesky(schur_block)  37.2 us
    another operation x6, other arithmetic, prepare(): lax.linalg.triangular_solve(factor_low, identity, left_side=True, lower=T...  31.8 us
    dot_general x8, matrix products, affinity(): lax.dot_general(row_data, block_rows, (((1,), (1,)), ((), ())), preferred...  29.9 us
    gather x1, local copies, waits for them, and re-layouts, per_device(): points = jnp.take(flat_rows, take_index, axis=0)  24.6 us
    dot_general x3, matrix products, extend(): lax.dot_general(factors, cross_rows, (((1,), (1,)), ((), ())), precision=...  21.4 us
  transfers between devices with their start and end apart: 4, of which 3 were waited for; matrix products, arithmetic and copies ran while one was open for 18% of the time, Pallas kernels for 0%

profile of v1, /device:TPU:1, one launch (start us, length us, event | category | flops | bytes accessed | tf_op | source)
XLA Modules:
  0.0 588.4 jit_solution(6224210699917319006)
XLA Ops:
  7.2 1.4 fusion.77
  10.6 0.7 compare_and_fusion.1
  11.3 0.7 fusion.66
  12.0 3.9 gather_fusion.2
  16.1 0.6 slice_select_fusion.2
  16.8 0.7 all-gather.9.cloned.1.call-update
  17.5 0.7 all-gather.11.cloned.1.call-update
  18.2 0.9 reduce_window_sum.11
  19.1 0.7 sub.107
  19.8 0.6 dynamic_slice.17
  20.4 0.6 dynamic_slice.16
  22.2 0.7 and_select_fusion.2
  23.2 58.2 %gather_fusion = bf16[16384,128]{1,0:T(8,128)(2,1)} fusion(bf16[16384,128]{1,0:T(8,128)(2,1)} %bitcast.112, s32[16384]{0:T(1024)S(1)} %broadcast_clamp_fusion), kind=kCustom, calls=%fused_computation | custom fusion | bytes 8454144 | tf_op jit(solution)/shard_map/jit(_take)/gather | solution.py:147
  81.4 7.6 %select_select_fusion = bf16[16,1024,128]{2,1,0:T(8,128)(2,1)} fusion(bf16[16,1024,128]{2,1,0:T(8,128)(2,1)} %bitcast.113, pred[16,1024]{1,0:T(8,128)(4,1)S(1)} %get-tuple-element.18, pred[16,1024]{1,0:T(8,128)(4,1)S(1)} %get-tuple-element.17), kind=kLoop, calls=%fused_computation.28 | loop fusion | flops 4194304 | bytes 8421376 | tf_op jit(solution)/shard_map/jit(_where)/select_n | solution.py:152
  89.1 10.1 %all-to-all-start = ((bf16[16,1024,128]{2,1,0:T(8,128)(2,1)}), bf16[16,1024,128]{2,1,0:T(8,128)(2,1)}, u32[]{:S(2)}, u32[]{:S(2)}) async-start(bf16[16,1024,128]{2,1,0:T(8,128)(2,1)} %select_select_fusion), calls=%async_computation | async-start | bytes 8388608 | tf_op jit(solution)/shard_map/all_to_all | solution.py:151
  99.2 0.6 gather_fusion.3
  100.6 105.9 %all-to-all-done = bf16[16,1024,128]{2,1,0:T(8,128)(2,1)} async-done(((bf16[16,1024,128]{2,1,0:T(8,128)(2,1)}), bf16[16,1024,128]{2,1,0:T(8,128)(2,1)}, u32[]{:S(2)}, u32[]{:S(2)}) %all-to-all-start) | async-done | bytes 4194336 | tf_op jit(solution)/shard_map/all_to_all | solution.py:151
  206.5 24.6 %gather_fusion.1 = bf16[8192,128]{1,0:T(8,128)(2,1)S(1)} fusion(bf16[16384,128]{1,0:T(8,128)(2,1)} %bitcast.7, s32[8192]{0:T(1024)S(1)} %broadcast_clamp_fusion.1), kind=kCustom, calls=%fused_computation.1 | custom fusion | bytes 4227072 | tf_op jit(solution)/shard_map/jit(_take)/gather | solution.py:159
  231.1 2.6 multiply_reduce_fusion
  233.7 4.7 reduce_sum.91
  238.4 63.4 %all-gather.9.cloned.1.call-done = bf16[32768,128]{1,0:T(8,128)(2,1)} async-done(((bf16[128,128]{1,0:T(8,128)(2,1)}), bf16[32768,128]{1,0:T(8,128)(2,1)}) %all-gather.9.cloned.1.call-update) | async-done | bytes 8388624 | tf_op jit(solution)/shard_map/all_gather | solution.py:13
  301.8 4.7 reduce_sum.92
  306.6 114.0 %all-gather.11.cloned.1.call-done = bf16[32768,128]{1,0:T(8,128)(2,1)} async-done(((bf16[128,128]{1,0:T(8,128)(2,1)}), bf16[32768,128]{1,0:T(8,128)(2,1)}) %all-gather.11.cloned.1.call-update) | async-done | bytes 8388624 | tf_op jit(solution)/shard_map/all_gather | solution.py:13
  420.5 4.7 reduce_sum.93
  425.8 9.6 %fusion.6 = f32[8192,128]{1,0:T(8,128)} fusion(bf16[128,128]{1,0:T(8,128)(2,1)S(1)} %reduce_sum.91, s32[128]{0:T(128)S(1)} %get-tuple-element.22, f32[128]{0:T(128)S(1)} %get-tuple-element.19, f32[8192]{0:T(1024)S(1)} %multiply_reduce_fusion, s32[8192]{0:T(1024)S(1)} %iota_add_fusion, bf16[8192,128]{1,0:T(8,128)(2,1)S(1)} %gather_fusion.1, ...), kind=kOutput, calls=%fused_computation.16 | convolution fusion | flops 276824064 | bytes 6398976 | tf_op jit(solution)/shard_map/dot_general | solution.py:21
  435.4 9.5 %fusion.9 = f32[8192,128]{1,0:T(8,128)} fusion(bf16[128,128]{1,0:T(8,128)(2,1)S(1)} %reduce_sum.92, s32[128]{0:T(128)S(1)} %get-tuple-element.24, f32[128]{0:T(128)S(1)} %get-tuple-element.21, f32[8192]{0:T(1024)S(1)} %multiply_reduce_fusion, s32[8192]{0:T(1024)S(1)} %iota_add_fusion, bf16[8192,128]{1,0:T(8,128)(2,1)S(1)} %gather_fusion.1, ...), kind=kOutput, calls=%fused_computation.19 | convolution fusion | flops 276824064 | bytes 6398976 | tf_op jit(solution)/shard_map/dot_general | solution.py:21
  445.1 9.8 %fusion.12 = f32[8192,128]{1,0:T(8,128)} fusion(bf16[128,128]{1,0:T(8,128)(2,1)S(1)} %reduce_sum.93, s32[128]{0:T(128)S(1)} %get-tuple-element.23, f32[128]{0:T(128)S(1)} %get-tuple-element.20, f32[8192]{0:T(1024)S(1)} %multiply_reduce_fusion, s32[8192]{0:T(1024)S(1)} %iota_add_fusion, bf16[8192,128]{1,0:T(8,128)(2,1)S(1)} %gather_fusion.1, ...), kind=kOutput, calls=%fused_computation.22 | convolution fusion | flops 276824064 | bytes 6398976 | tf_op jit(solution)/shard_map/dot_general | solution.py:21
  455.0 11.7 %cholesky.59 = f32[128,128]{1,0:T(8,128)S(1)} custom-call(f32[128,128]{1,0:T(8,128)S(1)} %fusion.54), custom_call_target="Cholesky" | custom-call | tf_op jit(solution)/shard_map/jit(cholesky)/cholesky | solution.py:78
  466.8 0.6 compare_reduce_fusion.2
  467.4 0.7 fusion.46
  468.1 9.8 %custom-call.9 = f32[1,128,128]{1,2,0:T(8,128)S(1)} custom-call(f32[1,128,128]{2,1,0:T(8,128)S(1)} %fusion.46), custom_call_target="InvertDiagBlocksLowerTriangular" | custom-call | tf_op jit(solution)/shard_map/triangular_solve/custom-call.0 | solution.py:79
  479.7 11.7 %cholesky.70 = f32[128,128]{1,0:T(8,128)S(1)} custom-call(f32[128,128]{1,0:T(8,128)S(1)} %fusion.52), custom_call_target="Cholesky" | custom-call | tf_op jit(solution)/shard_map/jit(cholesky)/cholesky | solution.py:78
  491.5 0.6 compare_reduce_fusion.1
  492.1 0.7 fusion.47
  492.8 10.2 %custom-call.10 = f32[1,128,128]{1,2,0:T(8,128)S(1)} custom-call(f32[1,128,128]{2,1,0:T(8,128)S(1)} %fusion.47), custom_call_target="InvertDiagBlocksLowerTriangular" | custom-call | tf_op jit(solution)/shard_map/triangular_solve/custom-call.0 | solution.py:79
  504.4 11.7 %cholesky.81 = f32[128,128]{1,0:T(8,128)S(1)} custom-call(f32[128,128]{1,0:T(8,128)S(1)} %fusion.50), custom_call_target="Cholesky" | custom-call | tf_op jit(solution)/shard_map/jit(cholesky)/cholesky | solution.py:78
  516.1 0.6 compare_reduce_fusion
  516.8 0.7 fusion.48
  517.4 9.8 %custom-call.11 = f32[1,128,128]{1,2,0:T(8,128)S(1)} custom-call(f32[1,128,128]{2,1,0:T(8,128)S(1)} %fusion.48), custom_call_target="InvertDiagBlocksLowerTriangular" | custom-call | tf_op jit(solution)/shard_map/triangular_solve/custom-call.0 | solution.py:79
  527.6 5.9 %fusion.78 = f32[8192,128]{0,1:T(8,128)S(1)} fusion(f32[8192,128]{1,0:T(8,128)} %fusion.6, f32[128,128]{1,0:T(8,128)S(1)} %fusion.41), kind=kOutput, calls=%fused_computation.174 | convolution fusion | flops 1610612736 | bytes 8454144 | tf_op jit(solution)/shard_map/dot_general | solution.py:39
  533.5 6.7 %convolution_subtract_fusion.1 = f32[8192,128]{1,0:T(8,128)S(1)} fusion(f32[8192,128]{1,0:T(8,128)S(1)} %copy-done, f32[8192,128]{0,1:T(8,128)S(1)} %fusion.78, f32[384,128]{0,1:T(8,128)S(1)} %fusion.79), kind=kOutput, calls=%fused_computation.9 | convolution fusion | flops 1611661312 | bytes 12648448 | tf_op jit(solution)/shard_map/dot_general | solution.py:32
  540.2 4.2 fusion.80
  544.4 14.2 %convolution_subtract_fusion = f32[8192,128]{1,0:T(8,128)S(1)} fusion(f32[8192,128]{1,0:T(8,128)S(1)} %copy-done.1, f32[8192,128]{0,1:T(8,128)S(1)} %fusion.80, f32[8192,128]{0,1:T(8,128)S(1)} %fusion.78, f32[384,128]{0,1:T(8,128)S(1)} %fusion.81, f32[384,128]{0,1:T(8,128)S(1)} %fusion.79), kind=kOutput, calls=%fused_computation.6 | convolution fusion | flops 3224403968 | bytes 17170432 | tf_op jit(solution)/shard_map/dot_general | solution.py:32
  558.7 4.4 fusion.82
  563.1 1.4 fusion
  565.2 0.6 broadcast_subtract_fusion
  565.8 7.0 %pad_maximum_fusion = bf16[1,1,8192,384]{2,3,1,0:T(8,128)(2,1)} fusion(bf16[1,1,8192,128]{2,3,1,0:T(8,128)(2,1)S(1)} %convert_bitcast_fusion, bf16[1,1,8192,128]{2,3,1,0:T(8,128)(2,1)S(1)} %convert_bitcast_fusion.1, bf16[1,1,8192,128]{2,3,1,0:T(8,128)(2,1)S(1)} %convert_bitcast_fusion.2), kind=kLoop, calls=%fused_computation.26 | loop fusion | flops 18874368 | bytes 12582912 | tf_op jit(solution)/shard_map/concatenate | solution.py:46
  572.8 8.6 %copy.32 = bf16[1,1,8192,384]{3,2,1,0:T(8,128)(2,1)} copy(bf16[1,1,8192,384]{2,3,1,0:T(8,128)(2,1)} %pad_maximum_fusion) | data formatting | bytes 12582912
  (61 shorter events, 6.3 us)
Async XLA Ops:
  7.2 226.5 %all-gather.7.cloned.1.call-start = ((), (), s32[]{:S(2)}) async-start(), calls=%async_computation.1 | async-start | bytes 8421376 | tf_op jit(solution)/shard_map/all_gather | solution.py:13
  16.7 285.1 %all-gather.9.cloned.1.call-start = ((), (), s32[]{:S(2)}) async-start(), calls=%async_computation.2 | async-start | bytes 8421376 | tf_op jit(solution)/shard_map/all_gather | solution.py:13
  17.5 403.0 %all-gather.11.cloned.1.call-start = ((), (), s32[]{:S(2)}) async-start(), calls=%async_computation.3 | async-start | bytes 8421376 | tf_op jit(solution)/shard_map/all_gather | solution.py:13
  89.1 10.1 %copy-start.3 = (s32[3]{0:T(128)S(1)}, s32[3]{0:T(128)}, u32[]{:S(2)}) copy-start(s32[3]{0:T(128)} %param.10) | copy-start | bytes 40
  89.1 11.2 %copy-start.2 = (s32[3,128]{1,0:T(4,128)S(1)}, s32[3,128]{1,0:T(4,128)}, u32[]{:S(2)}) copy-start(s32[3,128]{1,0:T(4,128)} %param.9) | copy-start | bytes 4612
  89.1 117.4 %all-to-all-start = ((bf16[16,1024,128]{2,1,0:T(8,128)(2,1)}), bf16[16,1024,128]{2,1,0:T(8,128)(2,1)}, u32[]{:S(2)}, u32[]{:S(2)}) async-start(bf16[16,1024,128]{2,1,0:T(8,128)(2,1)} %select_select_fusion), calls=%async_computation | async-start | bytes 8388608 | tf_op jit(solution)/shard_map/all_to_all | solution.py:151
  527.6 5.9 %copy-start = (f32[8192,128]{1,0:T(8,128)S(1)}, f32[8192,128]{1,0:T(8,128)}, u32[]{:S(2)}) copy-start(f32[8192,128]{1,0:T(8,128)} %fusion.9) | copy-start | bytes 12582916
  540.2 4.2 copy-start.1
Sparse Core Ops, SparseCore 0:
  16.9 156.3 all-gather.6
  176.9 124.8 all-gather.8
  305.5 114.9 all-gather.10
